TPU v7x, 32 devices: a whole 2x2x4 slice. The times are simulated.
32 devices in a mesh: fsdp: 8 (over z, y), rep: 4 (over x, core).
Axes of the slice: x: 2, y: 2, z: 4, core: 2. Of those that a mesh axis runs over, the one named last changes fastest.
Arguments:
- layer_input: bfloat16 [64, 512, 768], P(('fsdp', 'rep')), may hold values from -6 to 6
- segment_ids: int32 [64, 512], P(('fsdp', 'rep')), may hold values from 0 to 511, as said below
- joint_weight: bfloat16 [768, 2304], P('fsdp'), may hold values from -0.21875 to 0.21875
- query_bias: bfloat16 [768], replicated, may hold values from -3 to 3
- value_bias: bfloat16 [768], replicated, may hold values from -3 to 3
- close_weight: bfloat16 [768, 768], P('fsdp'), may hold values from -0.875 to 0.875
- close_bias: bfloat16 [768], replicated, may hold values from -3 to 3
- first_gain: bfloat16 [768], replicated, may hold values from 0.099609375 to 1.8984375
- first_shift: bfloat16 [768], replicated, may hold values from -3 to 3
- expand_weight: bfloat16 [768, 3072], P('fsdp'), may hold values from -0.21875 to 0.21875
- expand_bias: bfloat16 [3072], replicated, may hold values from -3 to 3
- shrink_weight: bfloat16 [3072, 768], P('fsdp'), may hold values from -0.109375 to 0.109375
- shrink_bias: bfloat16 [768], replicated, may hold values from -3 to 3
- second_gain: bfloat16 [768], replicated, may hold values from 0.099609375 to 1.8984375
- second_shift: bfloat16 [768], replicated, may hold values from -3 to 3
- cotangent: bfloat16 [64, 512, 768], P(('fsdp', 'rep')), may hold values from -6 to 6
Outputs:
- layer_output: bfloat16 [64, 512, 768], P(('fsdp', 'rep'))
- input_grad: float32 [64, 512, 768], P(('fsdp', 'rep'))
- joint_grad: float32 [768, 2304], P('fsdp')
- query_bias_grad: float32 [768], replicated
- value_bias_grad: float32 [768], replicated
- close_grad: float32 [768, 768], P('fsdp')
- close_bias_grad: float32 [768], replicated
- first_gain_grad: float32 [768], replicated
- first_shift_grad: float32 [768], replicated
- expand_grad: float32 [768, 3072], P('fsdp')
- expand_bias_grad: float32 [3072], replicated
- shrink_grad: float32 [3072, 768], P('fsdp')
- shrink_bias_grad: float32 [768], replicated
- second_gain_grad: float32 [768], replicated
- second_shift_grad: float32 [768], replicated
Inputs may be any that keep to these rules, and one draw needn't show every extreme that they name: `segment_ids`: along each packed row of 512 positions the document numbers start at 0, never fall and rise by at most one from a position to the next; every position belongs to a document. Some row holds 512 documents of one position.
All inputs are finite; a program needn't handle non-finite values.
Results may differ from a plain program's by a relative error of at most 0.015.
Values may be sent and summed in bfloat16 or wider, within the bound.
No kernel may reach another device: no remote copies, remote signals or barrier semaphores. Data moves between devices by JAX's collectives and lax.ppermute only.
A program may use at most 192 MiB of HBM per device.

v0:
```python
import math
import jax
import jax.numpy as jnp
from jax import lax
from jax.sharding import PartitionSpec as P

HEADS = 12
EPS = 1e-12


def layer_norm(values, gain, shift):
    average = jnp.mean(values, axis=-1, keepdims=True)
    centred = values - average
    variance = jnp.mean(centred * centred, axis=-1, keepdims=True)
    return centred * lax.rsqrt(variance + EPS) * gain + shift


def gelu_exact(values):
    return jax.nn.gelu(values, approximate=False)


def split_heads(packed):
    pos_count = packed.shape[0]
    model_width = packed.shape[1] // 3
    head_size = model_width // HEADS
    queries = packed[:, :model_width].reshape(pos_count, HEADS, head_size)
    keys_part = packed[:, model_width : 2 * model_width].reshape(pos_count, HEADS, head_size)
    values_part = packed[:, 2 * model_width :].reshape(pos_count, HEADS, head_size)
    return (queries, keys_part, values_part, 1.0 / math.sqrt(head_size))


def masked_scores(queries, keys_part, segments, score_scale):
    scores = (
        jnp.einsum("qhd,khd->hqk", queries, keys_part, preferred_element_type=jnp.float32)
        * score_scale
    )
    same_doc = segments[:, None] == segments[None, :]
    return jnp.where(same_doc[None], scores, -jnp.inf)


def attend_row(packed, segments):
    queries, keys_part, values_part, score_scale = split_heads(packed)
    scores = masked_scores(queries, keys_part, segments, score_scale)
    top_score = jnp.max(scores, axis=-1, keepdims=True)
    raised = jnp.exp(scores - top_score)
    denominator = jnp.sum(raised, axis=-1, keepdims=True)
    attn_low = (raised / denominator).astype(jnp.bfloat16)
    context = jnp.einsum("hqk,khd->qhd", attn_low, values_part, preferred_element_type=jnp.float32)
    return (
        context.reshape(packed.shape[0], packed.shape[1] // 3),
        top_score + jnp.log(denominator),
    )


def attend_back(packed, segments, log_total, grad_context):
    pos_count = packed.shape[0]
    model_width = packed.shape[1] // 3
    queries, keys_part, values_part, score_scale = split_heads(packed)
    scores = masked_scores(queries, keys_part, segments, score_scale)
    attn_weights = jnp.exp(scores - log_total)
    grad_heads = grad_context.reshape(pos_count, HEADS, model_width // HEADS)
    grad_attn = jnp.einsum(
        "qhd,khd->hqk", grad_heads, values_part, preferred_element_type=jnp.float32
    )
    inner_sum = jnp.sum(grad_attn * attn_weights, axis=-1, keepdims=True)
    grad_scores = (attn_weights * (grad_attn - inner_sum)).astype(jnp.bfloat16)
    grad_queries = (
        jnp.einsum("hqk,khd->qhd", grad_scores, keys_part, preferred_element_type=jnp.float32)
        * score_scale
    )
    grad_keys = (
        jnp.einsum("hqk,qhd->khd", grad_scores, queries, preferred_element_type=jnp.float32)
        * score_scale
    )
    grad_values = jnp.einsum(
        "hqk,qhd->khd",
        attn_weights.astype(jnp.bfloat16),
        grad_heads,
        preferred_element_type=jnp.float32,
    )
    return jnp.concatenate(
        [
            grad_queries.reshape(pos_count, model_width),
            grad_keys.reshape(pos_count, model_width),
            grad_values.reshape(pos_count, model_width),
        ],
        axis=1,
    )


def body(
    layer_input,
    segment_ids,
    joint_weight,
    query_bias,
    value_bias,
    close_weight,
    close_bias,
    first_gain,
    first_shift,
    expand_weight,
    expand_bias,
    shrink_weight,
    shrink_bias,
    second_gain,
    second_shift,
    cotangent,
):
    row_count, pos_count, model_width = layer_input.shape
    tok_count = row_count * pos_count
    flat_input = layer_input.reshape(tok_count, model_width)
    joint_full, close_full = (
        lax.all_gather(joint_weight, "fsdp", axis=0, tiled=True),
        lax.all_gather(close_weight, "fsdp", axis=0, tiled=True),
    )
    joint_bias = jnp.concatenate([query_bias, jnp.zeros_like(query_bias), value_bias]).astype(
        jnp.float32
    )
    mixed = jnp.dot(flat_input, joint_full, preferred_element_type=jnp.float32) + joint_bias
    joint_low = mixed.astype(jnp.bfloat16).reshape(row_count, pos_count, 3 * model_width)
    context, log_total = lax.map(
        lambda packet: attend_row(packet[0], packet[1]), (joint_low, segment_ids)
    )
    context_low = context.reshape(tok_count, model_width).astype(jnp.bfloat16)
    expand_full, shrink_full = (
        lax.all_gather(expand_weight, "fsdp", axis=0, tiled=True),
        lax.all_gather(shrink_weight, "fsdp", axis=0, tiled=True),
    )
    branch = jnp.dot(
        context_low, close_full, preferred_element_type=jnp.float32
    ) + close_bias.astype(jnp.float32)
    first_sum = flat_input.astype(jnp.float32) + branch
    hidden, first_pull = jax.vjp(
        layer_norm, first_sum, first_gain.astype(jnp.float32), first_shift.astype(jnp.float32)
    )
    hidden_low = hidden.astype(jnp.bfloat16)
    inner = jnp.dot(
        hidden_low, expand_full, preferred_element_type=jnp.float32
    ) + expand_bias.astype(jnp.float32)
    active, gelu_pull = jax.vjp(gelu_exact, inner)
    active_low = active.astype(jnp.bfloat16)
    ffn_out = jnp.dot(
        active_low, shrink_full, preferred_element_type=jnp.float32
    ) + shrink_bias.astype(jnp.float32)
    output, second_pull = jax.vjp(
        layer_norm,
        hidden + ffn_out,
        second_gain.astype(jnp.float32),
        second_shift.astype(jnp.float32),
    )
    layer_output = output.astype(jnp.bfloat16).reshape(row_count, pos_count, model_width)
    expand_back, shrink_back = (
        lax.all_gather(expand_weight, "fsdp", axis=0, tiled=True),
        lax.all_gather(shrink_weight, "fsdp", axis=0, tiled=True),
    )
    grad_second, second_gain_part, second_shift_part = second_pull(
        cotangent.reshape(tok_count, model_width).astype(jnp.float32)
    )
    grad_ffn = grad_second.astype(jnp.bfloat16)
    shrink_term = jnp.einsum("tf,td->fd", active_low, grad_ffn, preferred_element_type=jnp.float32)
    grad_active = jnp.einsum("td,fd->tf", grad_ffn, shrink_back, preferred_element_type=jnp.float32)
    grad_inner = gelu_pull(grad_active)[0].astype(jnp.bfloat16)
    expand_term = jnp.einsum(
        "td,tf->df", hidden_low, grad_inner, preferred_element_type=jnp.float32
    )
    grad_hidden = grad_second + jnp.einsum(
        "tf,df->td", grad_inner, expand_back, preferred_element_type=jnp.float32
    )
    expand_part, shrink_part = (
        lax.psum_scatter(expand_term, "fsdp", scatter_dimension=0, tiled=True),
        lax.psum_scatter(shrink_term, "fsdp", scatter_dimension=0, tiled=True),
    )
    grad_first, first_gain_part, first_shift_part = first_pull(grad_hidden)
    grad_branch = grad_first.astype(jnp.bfloat16)
    joint_back, close_back = (
        lax.all_gather(joint_weight, "fsdp", axis=0, tiled=True),
        lax.all_gather(close_weight, "fsdp", axis=0, tiled=True),
    )
    close_term = jnp.einsum(
        "td,te->de", context_low, grad_branch, preferred_element_type=jnp.float32
    )
    grad_context = jnp.einsum(
        "te,de->td", grad_branch, close_back, preferred_element_type=jnp.float32
    ).astype(jnp.bfloat16)
    grad_mixed = lax.map(
        lambda packet: attend_back(packet[0], packet[1], packet[2], packet[3]),
        (
            joint_low,
            segment_ids,
            log_total,
            grad_context.reshape(row_count, pos_count, model_width),
        ),
    )
    grad_mixed_low = grad_mixed.reshape(tok_count, 3 * model_width).astype(jnp.bfloat16)
    joint_term = jnp.einsum(
        "td,te->de", flat_input, grad_mixed_low, preferred_element_type=jnp.float32
    )
    input_grad = grad_first + jnp.einsum(
        "te,de->td", grad_mixed_low, joint_back, preferred_element_type=jnp.float32
    )
    joint_part, close_part = (
        lax.psum_scatter(joint_term, "fsdp", scatter_dimension=0, tiled=True),
        lax.psum_scatter(close_term, "fsdp", scatter_dimension=0, tiled=True),
    )
    joint_grad, close_grad, expand_grad, shrink_grad = (
        lax.psum(joint_part.astype(jnp.bfloat16), "rep").astype(jnp.float32),
        lax.psum(close_part.astype(jnp.bfloat16), "rep").astype(jnp.float32),
        lax.psum(expand_part.astype(jnp.bfloat16), "rep").astype(jnp.float32),
        lax.psum(shrink_part.astype(jnp.bfloat16), "rep").astype(jnp.float32),
    )
    grad_mixed_wide = grad_mixed_low.astype(jnp.float32)
    vector_terms = (
        jnp.sum(grad_mixed_wide[:, :model_width], axis=0),
        jnp.sum(grad_mixed_wide[:, 2 * model_width :], axis=0),
        jnp.sum(grad_branch.astype(jnp.float32), axis=0),
        first_gain_part,
        first_shift_part,
        jnp.sum(grad_inner.astype(jnp.float32), axis=0),
        jnp.sum(grad_ffn.astype(jnp.float32), axis=0),
        second_gain_part,
        second_shift_part,
    )
    (
        query_bias_grad,
        value_bias_grad,
        close_bias_grad,
        first_gain_grad,
        first_shift_grad,
        expand_bias_grad,
        shrink_bias_grad,
        second_gain_grad,
        second_shift_grad,
    ) = lax.psum(
        (
            vector_terms[0],
            vector_terms[1],
            vector_terms[2],
            vector_terms[3],
            vector_terms[4],
            vector_terms[5],
            vector_terms[6],
            vector_terms[7],
            vector_terms[8],
        ),
        ("fsdp", "rep"),
    )
    return (
        layer_output,
        input_grad.reshape(row_count, pos_count, model_width),
        joint_grad,
        query_bias_grad,
        value_bias_grad,
        close_grad,
        close_bias_grad,
        first_gain_grad,
        first_shift_grad,
        expand_grad,
        expand_bias_grad,
        shrink_grad,
        shrink_bias_grad,
        second_gain_grad,
        second_shift_grad,
    )


def solution(mesh):
    placed = (
        P(("fsdp", "rep"), None, None),
        P(("fsdp", "rep"), None),
        P("fsdp", None),
        P(),
        P(),
        P("fsdp", None),
        P(),
        P(),
        P(),
        P("fsdp", None),
        P(),
        P("fsdp", None),
        P(),
        P(),
        P(),
        P(("fsdp", "rep"), None, None),
    )
    return jax.shard_map(
        body,
        mesh=mesh,
        in_specs=placed,
        out_specs=(
            P(("fsdp", "rep"), None, None),
            P(("fsdp", "rep"), None, None),
            P("fsdp", None),
            P(),
            P(),
            P("fsdp", None),
            P(),
            P(),
            P(),
            P("fsdp", None),
            P(),
            P("fsdp", None),
            P(),
            P(),
            P(),
        ),
        check_vma=False,
    )
```

profile of v0, /device:TPU:0, one launch (start us, length us, event | category | flops | bytes accessed | tf_op | source)
XLA Modules:
  0.0 939.9 jit_solution(8562727655183991149)
XLA Ops:
  19.7 57.8 %all-gather.5.cloned.1.call-done = bf16[768,2304]{1,0:T(8,128)(2,1)} async-done(((bf16[96,2304]{1,0:T(8,128)(2,1)}), bf16[768,2304]{1,0:T(8,128)(2,1)}) %all-gather.5.cloned.1.call-update) | async-done | bytes 3538960 | tf_op jit(solution)/shard_map/all_gather | solution.py:113
  77.5 8.4 add_convert_fusion.1
  86.0 6.8 copy.54
  92.8 23.4 %while.22 = (s32[]{:T(128)}, bf16[2,512,768]{2,1,0:T(8,128)(2,1)}, f32[2,12,512,1]{2,1,3,0:T(8,128)S(1)}, bf16[2,512,2304]{1,2,0:T(8,128)(2,1)}, s32[2,512]{1,0:T(2,128)S(1)}, /*index=5*/s32[]{:T(128)}) while((s32[]{:T(128)}, bf16[2,512,768]{2,1,0:T(8,128)(2,1)}, f32[2,12,512,1]{2,1,3,0:T(8,128)S(1)}, bf16[2,512,2304]{1,2,0:T(8,128)(2,1)}, ...), condition=%wide.region_3.4_spmd, body=%wide.region_0.3_spmd.sunk | while | flops 843311104 | bytes 54753372 | solution.py:121
  99.6 3.6 fusion.98
  111.3 3.6 fusion.98
  116.2 3.4 all-gather.7.cloned.1.call-done
  119.6 3.8 fusion.33
  124.0 75.9 %all-gather.9.cloned.1.call-done = bf16[768,3072]{1,0:T(8,128)(2,1)} async-done(((bf16[96,3072]{1,0:T(8,128)(2,1)}), bf16[768,3072]{1,0:T(8,128)(2,1)}) %all-gather.9.cloned.1.call-update) | async-done | bytes 4718608 | tf_op jit(solution)/shard_map/all_gather | solution.py:126
  199.8 36.0 %multiply_convert_fusion.1 = (bf16[1024,3072]{1,0:T(8,128)(2,1)}, f32[1024,3072]{1,0:T(8,128)}, f32[1024,3072]{1,0:T(8,128)}) fusion(f32[3072]{0:T(1024)S(1)} %copy-done.28, bf16[768,3072]{1,0:T(8,128)(2,1)} %all-gather.9.cloned.1.call-done, f32[1024,768]{1,0:T(8,128)S(1)} %get-tuple-element.220, f32[768]{0:T(1024)S(1)} %copy-done.19, ...), kind=kOutput, calls=%fused_computation.34 | convolution fusion | flops 5043388416 | bytes 39348224 | tf_op jit(solution)/shard_map/dot_general | solution.py:137
  235.8 43.8 %all-gather.11.cloned.1.call-done = bf16[3072,768]{1,0:T(8,128)(2,1)} async-done(((bf16[384,768]{1,0:T(8,128)(2,1)}), bf16[3072,768]{1,0:T(8,128)(2,1)}) %all-gather.11.cloned.1.call-update) | async-done | bytes 4718608 | tf_op jit(solution)/shard_map/all_gather | solution.py:127
  279.6 8.9 fusion.34
  295.5 19.4 %convert_reduce_fusion = (f32[3072]{0:T(1024)}, bf16[1024,3072]{1,0:T(8,128)(2,1)}) fusion(f32[1024,3072]{1,0:T(8,128)} %get-tuple-element.207, bf16[1024,768]{1,0:T(8,128)(2,1)} %get-tuple-element.199, bf16[3072,768]{1,0:T(8,128)(2,1)} %all-gather.11.cloned.1.call-done, f32[1024,3072]{1,0:T(8,128)} %get-tuple-element.221, f32[3072]{0:T(1024)S(1)} %copy-done.28), kind=kOutput, calls=%fused_computation.32 | convolution fusion | flops 4885312512 | bytes 37773312 | tf_op jit(solution)/shard_map/td,fd->tf/dot_general | solution.py:161
  315.0 10.1 %multiply_reduce_fusion.1 = (f32[768]{0:T(1024)}, f32[1024]{0:T(1024)S(1)}, f32[768]{0:T(1024)}, f32[1024,768]{1,0:T(8,128)S(1)}) fusion(f32[1024,768]{1,0:T(8,128)S(1)} %get-tuple-element.220, f32[1024]{0:T(1024)S(1)} %fusion.22, f32[1024]{0:T(1024)S(1)} %broadcast_multiply_fusion.1, f32[768]{0:T(1024)S(1)} %copy-done.15, ...), kind=kOutput, calls=%fused_computation.62 | convolution fusion | flops 4839699456 | bytes 20472832 | tf_op jit(solution)/shard_map/tf,df->td/dot_general | solution.py:166
  334.9 62.1 %while.23 = (s32[]{:T(128)}, bf16[2,512,2304]{2,1,0:T(8,128)(2,1)}, bf16[2,512,2304]{1,2,0:T(8,128)(2,1)}, s32[2,512]{1,0:T(2,128)S(1)}, f32[2,12,512,1]{2,1,3,0...) while((s32[]{:T(128)}, bf16[2,512,2304]{2,1,0:T(8,128)(2,1)}, ...), condition=%wide.region_14.15_spmd, body=%wide.region_12.14_spmd.sunk | while | flops 2069358592 | bytes 142784688 | solution.py:185
  339.5 3.2 fusion.111
  342.7 6.9 multiply_reduce_fusion.6
  349.5 7.1 multiply_convert_fusion.3
  362.5 3.3 constant_dynamic-update-slice_fusion.5
  373.4 6.9 multiply_reduce_fusion.6
  380.3 7.2 multiply_convert_fusion.3
  393.4 3.4 constant_dynamic-update-slice_fusion.5
  397.0 9.7 %convolution_bitcast_fusion = f32[768,2304]{0,1:T(8,128)} fusion(bf16[2,512,2304]{2,1,0:T(8,128)(2,1)} %get-tuple-element.77, bf16[2,512,768]{2,1,0:T(8,128)(2,1)} %param.20), kind=kOutput, calls=%fused_computation.49 | convolution fusion | flops 3623878656 | bytes 13369344 | tf_op jit(solution)/shard_map/td,te->de/dot_general | solution.py:195
  406.7 8.1 copy.66
  416.6 10.7 %fusion.24 = f32[768,3072]{1,0:T(8,128)} fusion(bf16[1024,3072]{1,0:T(8,128)(2,1)} %get-tuple-element.226, f32[1024,768]{1,0:T(8,128)S(1)} %copy-done.1, f32[768]{0:T(1024)S(1)} %copy-done.20, f32[768]{0:T(1024)S(1)} %copy-done.16, f32[1024]{0:T(1024)S(1)} %copy-done.14, f32[1024]{0:T(1024)S(1)} %copy-done.12), kind=kOutput, calls=%fused_computation.89 | convolution fusion | flops 4835770368 | bytes 18888704 | tf_op jit(solution)/shard_map/td,tf->df/dot_general | solution.py:163
  428.7 10.2 %fusion.37 = f32[3072,768]{1,0:T(8,128)} fusion(bf16[1024,3072]{1,0:T(8,128)(2,1)} %get-tuple-element.206, bf16[1024,768]{1,0:T(8,128)(2,1)S(1)} %copy-done.8), kind=kOutput, calls=%fused_computation.99 | convolution fusion | flops 4831838208 | bytes 17301504 | tf_op jit(solution)/shard_map/tf,td->fd/dot_general | solution.py:160
  444.5 43.5 %all-reduce = (f32[768]{0:T(1024)}, f32[768]{0:T(1024)}, f32[768]{0:T(1024)}, f32[768]{0:T(1024)}, f32[768]{0:T(1024)}, /*index=5*/f32[3072]{0:T(1024)}, f32[768]{0:T(1024)}, f32[768]{0:T(1024)}, f32[768]{0:T(1024)}) all-reduce(f32[768]{0:T(1024)S(1)} %get-tuple-element.157, ...), channel_id=1, replica_groups=mesh['fsdp'=8,'rep'=4] {'fsdp','rep'}, use_global_device_ids=true, to_apply=%region_18.19 | all-reduce | flops 9216 | bytes 73728 | tf_op jit(solution)/shard_map/psum | solution.py:233
  489.6 54.0 %reduce-scatter.13.cloned.1.call-done = f32[96,2304]{1,0:T(8,128)} async-done(((f32[768,2304]{1,0:T(8,128)}), f32[96,2304]{1,0:T(8,128)}) %reduce-scatter.13.cloned.1.call-update) | async-done | bytes 884752
  545.9 162.6 %reduce-scatter.9.cloned.1.call-done = f32[96,3072]{1,0:T(8,128)} async-done(((f32[768,3072]{1,0:T(8,128)}), f32[96,3072]{1,0:T(8,128)}) %reduce-scatter.9.cloned.1.call-update) | async-done | bytes 1179664 | tf_op jit(solution)/shard_map/reduce_scatter | solution.py:170
  710.6 162.7 %reduce-scatter.11.cloned.1.call-done = f32[384,768]{1,0:T(8,128)} async-done(((f32[3072,768]{1,0:T(8,128)}), f32[384,768]{1,0:T(8,128)}) %reduce-scatter.11.cloned.1.call-update) | async-done | bytes 1179664 | tf_op jit(solution)/shard_map/reduce_scatter | solution.py:171
  875.5 8.9 add_add_fusion.4
  884.5 40.4 %all-reduce.4.cloned.1.call-done = (bf16[96,2304]{0,1:T(8,128)(2,1)}, bf16[96,768]{1,0:T(8,128)(2,1)}, bf16[96,3072]{1,0:T(8,128)(2,1)}, bf16[384,768]{1,0:T(8,128)(2,1)}) async-done(((bf16[96,2304]{0,1:T(8,128)(2,1)}, bf16[96,768]{1,0:T(8,128)(2,1)}, bf16[96,3072]{1,0:T(8,128)(2,1)}, bf16[384,768]{1,0:T(8,128)(2,1)}), (bf16[96,2304]{0,1:T(8,128)(2,1)}, bf16[96,768]{1,0:T(8,128)(2,1)}, ...) | async-done | bytes 1769488 | tf_op jit(solution)/shard_map/psum | solution.py:206
  (176 shorter events, 94.5 us)
Async XLA Ops:
  7.2 70.3 %all-gather.5.cloned.1.call-start = ((), (), s32[]{:S(2)}) async-start(), calls=%async_computation.4 | async-start | bytes 3981312 | tf_op jit(solution)/shard_map/all_gather | solution.py:113
  7.9 111.7 %all-gather.7.cloned.1.call-start = ((), (), s32[]{:S(2)}) async-start(), calls=%async_computation.5 | async-start | bytes 1327104 | tf_op jit(solution)/shard_map/all_gather | solution.py:114
  8.7 191.2 %all-gather.9.cloned.1.call-start = ((), (), s32[]{:S(2)}) async-start(), calls=%async_computation.6 | async-start | bytes 5308416 | tf_op jit(solution)/shard_map/all_gather | solution.py:126
  9.4 270.2 %all-gather.11.cloned.1.call-start = ((), (), s32[]{:S(2)}) async-start(), calls=%async_computation.7 | async-start | bytes 5308416 | tf_op jit(solution)/shard_map/all_gather | solution.py:127
  10.0 478.0 %reduce-scatter.7.cloned.1.call-start = ((), (), s32[]{:S(2)}) async-start(), calls=%async_computation.8 | async-start | bytes 2654208 | tf_op jit(solution)/shard_map/reduce_scatter | solution.py:203
  86.0 6.8 copy-start.17
  92.8 26.8 %copy-start.31 = (f32[768]{0:T(1024)S(1)}, f32[768]{0:T(1024)}, u32[]{:S(2)}) copy-start(f32[768]{0:T(1024)} %convert_element_type.127) | copy-start | bytes 9220
  116.2 3.4 copy-start.9
  119.6 80.2 %copy-start.15 = (f32[768]{0:T(1024)S(1)}, f32[768]{0:T(1024)}, u32[]{:S(2)}) copy-start(f32[768]{0:T(1024)} %convert_element_type.128) | copy-start | bytes 9220
  119.6 80.2 %copy-start.19 = (f32[768]{0:T(1024)S(1)}, f32[768]{0:T(1024)}, u32[]{:S(2)}) copy-start(f32[768]{0:T(1024)} %convert_element_type.129) | copy-start | bytes 9220
  119.6 80.2 %copy-start.28 = (f32[3072]{0:T(1024)S(1)}, f32[3072]{0:T(1024)}, u32[]{:S(2)}) copy-start(f32[3072]{0:T(1024)} %convert_element_type.131) | copy-start | bytes 36868
  123.4 201.7 %copy-start = (f32[1024,768]{1,0:T(8,128)}, f32[1024,768]{1,0:T(8,128)S(1)}, u32[]{:S(2)}) copy-start(f32[1024,768]{1,0:T(8,128)S(1)} %get-tuple-element.220) | copy-start | bytes 9437188
  123.4 201.7 %copy-start.11 = (f32[1024]{0:T(1024)}, f32[1024]{0:T(1024)S(1)}, u32[]{:S(2)}) copy-start(f32[1024]{0:T(1024)S(1)} %broadcast_multiply_fusion.1) | copy-start | bytes 12292
  123.9 201.2 %copy-start.13 = (f32[1024]{0:T(1024)}, f32[1024]{0:T(1024)S(1)}, u32[]{:S(2)}) copy-start(f32[1024]{0:T(1024)S(1)} %fusion.22) | copy-start | bytes 12292
  123.9 155.6 %copy-start.30 = (f32[768]{0:T(1024)S(1)}, f32[768]{0:T(1024)}, u32[]{:S(2)}) copy-start(f32[768]{0:T(1024)} %convert_element_type.133) | copy-start | bytes 9220
  279.6 9.5 %copy-start.2 = (bf16[2,512,768]{2,1,0:T(8,128)(2,1)S(1)}, bf16[2,512,768]{2,1,0:T(8,128)(2,1)}, u32[]{:S(2)}) copy-start(bf16[2,512,768]{2,1,0:T(8,128)(2,1)} %param.35) | copy-start | bytes 4718596
  279.6 9.5 %copy-start.21 = (f32[768]{0:T(1024)S(1)}, f32[768]{0:T(1024)}, u32[]{:S(2)}) copy-start(f32[768]{0:T(1024)} %convert_element_type.134) | copy-start | bytes 9220
  288.5 2.3 copy-start.24
  326.6 2.6 copy-start.34
  326.6 2.6 copy-start.22
  332.1 2.8 copy-start.10
  332.1 2.8 copy-start.18
  332.1 211.5 %reduce-scatter.13.cloned.1.call-start = ((), (), s32[]{:S(2)}) async-start(), calls=%async_computation.11 | async-start | bytes 7962624
  335.0 2.6 copy-start.6
  362.5 3.3 copy-start.7
  365.8 2.6 copy-start.6
  393.3 3.4 copy-start.7
  414.8 293.7 %reduce-scatter.9.cloned.1.call-start = ((), (), s32[]{:S(2)}) async-start(), calls=%async_computation.9 | async-start | bytes 10616832 | tf_op jit(solution)/shard_map/reduce_scatter | solution.py:170
  427.3 446.0 %reduce-scatter.11.cloned.1.call-start = ((), (), s32[]{:S(2)}) async-start(), calls=%async_computation.10 | async-start | bytes 10616832 | tf_op jit(solution)/shard_map/reduce_scatter | solution.py:171
  438.9 485.9 %all-reduce.4.cloned.1.call-start = ((), (), s32[]{:S(2)}) async-start(), calls=%async_computation.12 | async-start | bytes 3833856 | tf_op jit(solution)/shard_map/psum | solution.py:206
  444.2 431.3 %copy-start.5 = (f32[1024,768]{1,0:T(8,128)S(1)}, f32[1024,768]{1,0:T(8,128)}, u32[]{:S(2)}) copy-start(f32[1024,768]{1,0:T(8,128)} %copy-done.4) | copy-start | bytes 9437188
  444.2 431.3 %copy-start.23 = (f32[1024]{0:T(1024)S(1)}, f32[1024]{0:T(1024)}, u32[]{:S(2)}) copy-start(f32[1024]{0:T(1024)} %copy-done.22) | copy-start | bytes 12292
  (14 other events, 18.2 us)
Sparse Core Ops, SparseCore 0:
  10.2 67.3 all-gather.4
  79.7 39.8 all-gather.6
  121.8 78.0 all-gather.8
  201.9 77.6 all-gather.10
  332.2 67.9 reduce-scatter.6
  414.9 128.6 reduce-scatter.12
  547.2 161.2 reduce-scatter.8
  712.1 161.1 reduce-scatter.10
  877.1 47.7 all-reduce.3
where the time goes:
time: 944 us; the launch traced here: 940 us
  waiting for transfers between devices  603 us (64%)
  matrix products  173 us (18%)
  other arithmetic  55.7 us (6%)
  local copies, waits for them, and re-layouts  48.9 us (5%)
  blocking collectives  43.5 us (5%)
  between operations  14.5 us (2%)
    reduce_scatter x1, waiting for transfers between devices, body(): lax.psum_scatter(shrink_term, 'fsdp', scatter_dimension=0, tiled=True)  163 us
    reduce_scatter x1, waiting for transfers between devices, body(): lax.psum_scatter(expand_term, 'fsdp', scatter_dimension=0, tiled=True)  163 us
    all_gather x1, waiting for transfers between devices, body(): lax.all_gather(expand_weight, 'fsdp', axis=0, tiled=True)  75.9 us
    all_gather x1, waiting for transfers between devices, body(): lax.all_gather(joint_weight, 'fsdp', axis=0, tiled=True)  57.8 us
    unnamed x10, waiting for transfers between devices  56.7 us
    all_gather x1, waiting for transfers between devices, body(): lax.all_gather(shrink_weight, 'fsdp', axis=0, tiled=True)  43.8 us
    psum x1, blocking collectives, body(): lax.psum((vector_terms[0], vector_terms[1], vector_terms[2], vector_terms...  43.5 us
    psum x1, waiting for transfers between devices, body(): lax.psum(joint_part.astype(jnp.bfloat16), 'rep').astype(jnp.float32)  40.4 us
  transfers between devices with their start and end apart: 9, of which 8 were waited for; matrix products, arithmetic and copies ran while one was open for 22% of the time, Pallas kernels for 0%

commit v1 on v0

--- a/solution.py
+++ b/solution.py
@@ -123,7 +123,9 @@
     )
     context_low = context.reshape(tok_count, model_width).astype(jnp.bfloat16)
     expand_full, shrink_full = (
-        lax.all_gather(expand_weight, "fsdp", axis=0, tiled=True),
+        jnp.concatenate(
+            lax.all_to_all(jnp.stack([expand_weight] * lax.axis_size("fsdp")), "fsdp", 0, 0), axis=0
+        ),
         lax.all_gather(shrink_weight, "fsdp", axis=0, tiled=True),
     )
     branch = jnp.dot(

time: 944 us -> 1010 us (1.070)
  waiting for transfers between devices: 603 us -> 644 us
    all_gather x1, waiting for transfers between devices: 57.8 us -> 133 us  [body(): lax.all_gather(joint_weight, 'fsdp', axis=0, tiled=True)]
    all_gather x1, waiting for transfers between devices: 75.9 us -> 44.7 us  [body(): lax.all_gather(expand_weight, 'fsdp', axis=0, tiled=True)]
    dot_general x1, matrix products: 10.1 us -> 21.2 us  [body(): jnp.einsum('tf,df->td', grad_inner, expand_back, preferred_element_type=j...]
    unnamed x69 -> x93, local copies, waits for them, and re-layouts: 19.1 us -> 21.9 us
  transfers between devices with their start and end apart: 9 -> 10, of which waited for: 8 -> 8; matrix products, arithmetic and copies ran while one was open for 22% -> 24% of each run, Pallas kernels for 0% -> 0%
where the time goes in v1:
time: 1010 us; the launch traced here: 996 us
  waiting for transfers between devices  644 us (64%)
  matrix products  181 us (18%)
  local copies, waits for them, and re-layouts  55.5 us (5%)
  other arithmetic  49.1 us (5%)
  blocking collectives  43.5 us (4%)
  between operations  14.8 us (1%)
    reduce_scatter x1, waiting for transfers between devices, body(): lax.psum_scatter(shrink_term, 'fsdp', scatter_dimension=0, tiled=True)  163 us
    reduce_scatter x1, waiting for transfers between devices, body(): lax.psum_scatter(expand_term, 'fsdp', scatter_dimension=0, tiled=True)  163 us
    all_gather x1, waiting for transfers between devices, body(): lax.all_gather(joint_weight, 'fsdp', axis=0, tiled=True)  133 us
    unnamed x10, waiting for transfers between devices  56.7 us
    all_gather x1, waiting for transfers between devices, body(): lax.all_gather(expand_weight, 'fsdp', axis=0, tiled=True)  44.7 us
    psum x1, blocking collectives, body(): lax.psum((vector_terms[0], vector_terms[1], vector_terms[2], vector_terms...  43.5 us
    psum x1, waiting for transfers between devices, body(): lax.psum(joint_part.astype(jnp.bfloat16), 'rep').astype(jnp.float32)  40.4 us
    all_gather x1, waiting for transfers between devices, body(): lax.all_gather(shrink_weight, 'fsdp', axis=0, tiled=True)  39.5 us
  transfers between devices with their start and end apart: 10, of which 8 were waited for; matrix products, arithmetic and copies ran while one was open for 24% of the time, Pallas kernels for 0%

profile of v1, /device:TPU:0, one launch (start us, length us, event | category | flops | bytes accessed | tf_op | source)
XLA Modules:
  0.0 996.4 jit_solution(12374983142267435396)
XLA Ops:
  10.0 3.8 stack.2
  13.8 7.5 all-to-all-start
  25.6 133.2 %all-gather.5.cloned.1.call-done = bf16[768,2304]{1,0:T(8,128)(2,1)} async-done(((bf16[96,2304]{1,0:T(8,128)(2,1)}), bf16[768,2304]{1,0:T(8,128)(2,1)}) %all-gather.5.cloned.1.call-update) | async-done | bytes 3538960 | tf_op jit(solution)/shard_map/all_gather | solution.py:113
  158.8 7.5 add_convert_fusion.1
  166.3 6.7 copy.54
  173.0 23.4 %while.22 = (s32[]{:T(128)}, bf16[2,512,768]{2,1,0:T(8,128)(2,1)}, f32[2,12,512,1]{2,1,3,0:T(8,128)S(1)}, bf16[2,512,2304]{1,2,0:T(8,128)(2,1)}, s32[2,512]{1,0:T(2,128)S(1)}, /*index=5*/s32[]{:T(128)}) while((s32[]{:T(128)}, bf16[2,512,768]{2,1,0:T(8,128)(2,1)}, f32[2,12,512,1]{2,1,3,0:T(8,128)S(1)}, bf16[2,512,2304]{1,2,0:T(8,128)(2,1)}, ...), condition=%wide.region_3.4_spmd, body=%wide.region_0.3_spmd.sunk | while | flops 843311104 | bytes 54753372 | solution.py:121
  179.9 3.6 fusion.98
  191.5 3.6 fusion.98
  196.4 3.9 all-gather.7.cloned.1.call-done
  200.3 3.8 fusion.33
  204.7 36.4 %multiply_convert_fusion.1 = (bf16[1024,3072]{1,0:T(8,128)(2,1)}, f32[1024,3072]{1,0:T(8,128)}, f32[1024,3072]{1,0:T(8,128)}) fusion(f32[3072]{0:T(1024)S(1)} %copy-done.30, bf16[768,3072]{1,0:T(8,128)(2,1)} %bitcast.25, f32[1024,768]{1,0:T(8,128)S(1)} %get-tuple-element.220, f32[768]{0:T(1024)S(1)} %copy-done.21, f32[768]{0:T(1024)S(1)} %copy-done.17, ...), kind=kOutput, calls=%fused_computation.34 | convolution fusion | flops 5043388416 | bytes 39348224 | tf_op jit(solution)/shard_map/dot_general | solution.py:139
  241.1 39.5 %all-gather.9.cloned.1.call-done = bf16[3072,768]{1,0:T(8,128)(2,1)} async-done(((bf16[384,768]{1,0:T(8,128)(2,1)}), bf16[3072,768]{1,0:T(8,128)(2,1)}) %all-gather.9.cloned.1.call-update) | async-done | bytes 4718608 | tf_op jit(solution)/shard_map/all_gather | solution.py:129
  280.6 8.9 fusion.34
  298.2 17.4 %convert_reduce_fusion = (f32[3072]{0:T(1024)}, bf16[1024,3072]{1,0:T(8,128)(2,1)}) fusion(f32[1024,3072]{1,0:T(8,128)} %get-tuple-element.207, bf16[1024,768]{1,0:T(8,128)(2,1)S(1)} %get-tuple-element.199, bf16[3072,768]{1,0:T(8,128)(2,1)} %all-gather.9.cloned.1.call-done, f32[1024,3072]{1,0:T(8,128)} %get-tuple-element.221, f32[3072]{0:T(1024)S(1)} %copy-done.30), kind=kOutput, calls=%fused_computation.32 | convolution fusion | flops 4885312512 | bytes 37773312 | tf_op jit(solution)/shard_map/td,fd->tf/dot_general | solution.py:163
  315.6 44.7 %all-gather.11.cloned.1.call-done = bf16[768,3072]{1,0:T(8,128)(2,1)} async-done(((bf16[96,3072]{1,0:T(8,128)(2,1)}), bf16[768,3072]{1,0:T(8,128)(2,1)}) %all-gather.11.cloned.1.call-update) | async-done | bytes 4718608 | tf_op jit(solution)/shard_map/all_gather | solution.py:155
  360.3 21.2 %multiply_reduce_fusion.1 = (f32[768]{0:T(1024)}, f32[1024]{0:T(1024)S(1)}, f32[768]{0:T(1024)}, f32[1024,768]{1,0:T(8,128)S(1)}) fusion(f32[1024,768]{1,0:T(8,128)S(1)} %get-tuple-element.220, f32[1024]{0:T(1024)S(1)} %fusion.22, f32[1024]{0:T(1024)S(1)} %broadcast_multiply_fusion.1, f32[768]{0:T(1024)S(1)} %copy-done.17, ...), kind=kOutput, calls=%fused_computation.62 | convolution fusion | flops 4839699456 | bytes 20472832 | tf_op jit(solution)/shard_map/tf,df->td/dot_general | solution.py:168
  391.3 61.9 %while.23 = (s32[]{:T(128)}, bf16[2,512,2304]{2,1,0:T(8,128)(2,1)}, bf16[2,512,2304]{1,2,0:T(8,128)(2,1)}, s32[2,512]{1,0:T(2,128)S(1)}, f32[2,12,512,1]{2,1,3,0...) while((s32[]{:T(128)}, bf16[2,512,2304]{2,1,0:T(8,128)(2,1)}, ...), condition=%wide.region_14.15_spmd, body=%wide.region_12.14_spmd.sunk | while | flops 2069358592 | bytes 142784688 | solution.py:187
  399.0 6.8 multiply_reduce_fusion.6
  405.8 7.1 multiply_convert_fusion.3
  418.8 3.4 constant_dynamic-update-slice_fusion.5
  429.8 6.8 multiply_reduce_fusion.6
  436.6 7.2 multiply_convert_fusion.3
  453.2 9.7 convolution_bitcast_fusion
  463.0 8.1 copy.66
  472.9 10.6 %fusion.24 = f32[768,3072]{1,0:T(8,128)} fusion(bf16[1024,3072]{1,0:T(8,128)(2,1)} %get-tuple-element.226, f32[1024,768]{1,0:T(8,128)S(1)} %copy-done.1, f32[768]{0:T(1024)S(1)} %copy-done.22, f32[768]{0:T(1024)S(1)} %copy-done.18, f32[1024]{0:T(1024)S(1)} %copy-done.16, f32[1024]{0:T(1024)S(1)} %copy-done.14), kind=kOutput, calls=%fused_computation.89 | convolution fusion | flops 4835770368 | bytes 18888704 | tf_op jit(solution)/shard_map/td,tf->df/dot_general | solution.py:165
  485.0 10.2 %fusion.37 = f32[3072,768]{1,0:T(8,128)} fusion(bf16[1024,3072]{1,0:T(8,128)(2,1)} %get-tuple-element.206, bf16[1024,768]{1,0:T(8,128)(2,1)S(1)} %copy-done.10), kind=kOutput, calls=%fused_computation.99 | convolution fusion | flops 4831838208 | bytes 17301504 | tf_op jit(solution)/shard_map/tf,td->fd/dot_general | solution.py:162
  500.8 43.5 %all-reduce = (f32[768]{0:T(1024)}, f32[768]{0:T(1024)}, f32[768]{0:T(1024)}, f32[768]{0:T(1024)}, f32[768]{0:T(1024)}, /*index=5*/f32[3072]{0:T(1024)}, f32[768]{0:T(1024)}, f32[768]{0:T(1024)}, f32[768]{0:T(1024)}) all-reduce(f32[768]{0:T(1024)S(1)} %get-tuple-element.157, ...), channel_id=1, replica_groups=mesh['fsdp'=8,'rep'=4] {'fsdp','rep'}, use_global_device_ids=true, to_apply=%region_18.19 | all-reduce | flops 9216 | bytes 73728 | tf_op jit(solution)/shard_map/psum | solution.py:235
  546.0 54.0 %reduce-scatter.13.cloned.1.call-done = f32[96,2304]{1,0:T(8,128)} async-done(((f32[768,2304]{1,0:T(8,128)}), f32[96,2304]{1,0:T(8,128)}) %reduce-scatter.13.cloned.1.call-update) | async-done | bytes 884752
  602.2 162.6 %reduce-scatter.9.cloned.1.call-done = f32[96,3072]{1,0:T(8,128)} async-done(((f32[768,3072]{1,0:T(8,128)}), f32[96,3072]{1,0:T(8,128)}) %reduce-scatter.9.cloned.1.call-update) | async-done | bytes 1179664 | tf_op jit(solution)/shard_map/reduce_scatter | solution.py:172
  767.0 162.7 %reduce-scatter.11.cloned.1.call-done = f32[384,768]{1,0:T(8,128)} async-done(((f32[3072,768]{1,0:T(8,128)}), f32[384,768]{1,0:T(8,128)}) %reduce-scatter.11.cloned.1.call-update) | async-done | bytes 1179664 | tf_op jit(solution)/shard_map/reduce_scatter | solution.py:173
  931.8 9.0 add_add_fusion.4
  940.8 40.4 %all-reduce.4.cloned.1.call-done = (bf16[96,2304]{0,1:T(8,128)(2,1)}, bf16[96,768]{1,0:T(8,128)(2,1)}, bf16[96,3072]{1,0:T(8,128)(2,1)}, bf16[384,768]{1,0:T(8,128)(2,1)}) async-done(((bf16[96,2304]{0,1:T(8,128)(2,1)}, bf16[96,768]{1,0:T(8,128)(2,1)}, bf16[96,3072]{1,0:T(8,128)(2,1)}, bf16[384,768]{1,0:T(8,128)(2,1)}), (bf16[96,2304]{0,1:T(8,128)(2,1)}, bf16[96,768]{1,0:T(8,128)(2,1)}, ...) | async-done | bytes 1769488 | tf_op jit(solution)/shard_map/psum | solution.py:208
  (203 shorter events, 97.4 us)
Async XLA Ops:
  7.2 151.6 %all-gather.5.cloned.1.call-start = ((), (), s32[]{:S(2)}) async-start(), calls=%async_computation.5 | async-start | bytes 3981312 | tf_op jit(solution)/shard_map/all_gather | solution.py:113
  7.9 192.4 %all-gather.7.cloned.1.call-start = ((), (), s32[]{:S(2)}) async-start(), calls=%async_computation.6 | async-start | bytes 1327104 | tf_op jit(solution)/shard_map/all_gather | solution.py:114
  8.7 271.9 %all-gather.9.cloned.1.call-start = ((), (), s32[]{:S(2)}) async-start(), calls=%async_computation.7 | async-start | bytes 5308416 | tf_op jit(solution)/shard_map/all_gather | solution.py:129
  9.4 350.9 %all-gather.11.cloned.1.call-start = ((), (), s32[]{:S(2)}) async-start(), calls=%async_computation.8 | async-start | bytes 5308416 | tf_op jit(solution)/shard_map/all_gather | solution.py:155
  13.7 7.6 copy-start.37
  13.7 8.2 copy-start.38
  13.7 8.8 copy-start.39
  13.7 9.4 copy-start.40
  13.7 10.0 %copy-start.41 = (bf16[768]{0:T(1024)(128)(2,1)S(1)}, bf16[768]{0:T(1024)(128)(2,1)}, u32[]{:S(2)}) copy-start(bf16[768]{0:T(1024)(128)(2,1)} %param.32) | copy-start | bytes 4612
  13.7 10.6 %copy-start.42 = (bf16[768]{0:T(1024)(128)(2,1)S(1)}, bf16[768]{0:T(1024)(128)(2,1)}, u32[]{:S(2)}) copy-start(bf16[768]{0:T(1024)(128)(2,1)} %param.34) | copy-start | bytes 4612
  13.8 11.2 %copy-start.32 = (bf16[3072]{0:T(1024)(128)(2,1)S(1)}, bf16[3072]{0:T(1024)(128)(2,1)}, u32[]{:S(2)}) copy-start(bf16[3072]{0:T(1024)(128)(2,1)} %param.30) | copy-start | bytes 18436
  13.8 11.8 %copy-start.43 = (bf16[768]{0:T(1024)(128)(2,1)S(1)}, bf16[768]{0:T(1024)(128)(2,1)}, u32[]{:S(2)}) copy-start(bf16[768]{0:T(1024)(128)(2,1)} %param.24) | copy-start | bytes 4612
  13.8 11.8 %copy-start.44 = (bf16[768]{0:T(1024)(128)(2,1)S(1)}, bf16[768]{0:T(1024)(128)(2,1)}, u32[]{:S(2)}) copy-start(bf16[768]{0:T(1024)(128)(2,1)} %param.23) | copy-start | bytes 4612
  13.8 145.0 %copy-start.45 = (bf16[2,512,768]{2,1,0:T(8,128)(2,1)S(1)}, bf16[2,512,768]{2,1,0:T(8,128)(2,1)}, u32[]{:S(2)}) copy-start(bf16[2,512,768]{2,1,0:T(8,128)(2,1)} %param.20) | copy-start | bytes 4718596
  13.8 190.8 %all-to-all-start = ((bf16[8,96,3072]{2,1,0:T(8,128)(2,1)}), bf16[8,96,3072]{2,1,0:T(8,128)(2,1)}, u32[]{:S(2)}, u32[]{:S(2)}) async-start(bf16[8,96,3072]{2,1,0:T(8,128)(2,1)} %stack.2), calls=%async_computation | async-start | bytes 9437184 | tf_op jit(solution)/shard_map/all_to_all | solution.py:127
  21.3 523.0 %reduce-scatter.7.cloned.1.call-start = ((), (), s32[]{:S(2)}) async-start(), calls=%async_computation.9 | async-start | bytes 2654208 | tf_op jit(solution)/shard_map/reduce_scatter | solution.py:205
  166.3 6.7 copy-start.19
  173.0 27.3 %copy-start.34 = (f32[768]{0:T(1024)S(1)}, f32[768]{0:T(1024)}, u32[]{:S(2)}) copy-start(f32[768]{0:T(1024)} %convert_element_type.127) | copy-start | bytes 9220
  200.3 4.4 copy-start.21
  200.3 4.4 copy-start.30
  204.1 177.5 %copy-start = (f32[1024,768]{1,0:T(8,128)}, f32[1024,768]{1,0:T(8,128)S(1)}, u32[]{:S(2)}) copy-start(f32[1024,768]{1,0:T(8,128)S(1)} %get-tuple-element.220) | copy-start | bytes 9437188
  204.1 177.4 %copy-start.13 = (f32[1024]{0:T(1024)}, f32[1024]{0:T(1024)S(1)}, u32[]{:S(2)}) copy-start(f32[1024]{0:T(1024)S(1)} %broadcast_multiply_fusion.1) | copy-start | bytes 12292
  204.6 176.9 %copy-start.15 = (f32[1024]{0:T(1024)}, f32[1024]{0:T(1024)S(1)}, u32[]{:S(2)}) copy-start(f32[1024]{0:T(1024)S(1)} %fusion.22) | copy-start | bytes 12292
  204.7 75.9 %copy-start.33 = (f32[768]{0:T(1024)S(1)}, f32[768]{0:T(1024)}, u32[]{:S(2)}) copy-start(f32[768]{0:T(1024)} %convert_element_type.133) | copy-start | bytes 9220
  280.6 9.5 copy-start.2
  280.6 9.5 copy-start.23
  388.6 211.4 %reduce-scatter.13.cloned.1.call-start = ((), (), s32[]{:S(2)}) async-start(), calls=%async_computation.12 | async-start | bytes 7962624
  471.1 293.7 %reduce-scatter.9.cloned.1.call-start = ((), (), s32[]{:S(2)}) async-start(), calls=%async_computation.10 | async-start | bytes 10616832 | tf_op jit(solution)/shard_map/reduce_scatter | solution.py:172
  483.6 446.0 %reduce-scatter.11.cloned.1.call-start = ((), (), s32[]{:S(2)}) async-start(), calls=%async_computation.11 | async-start | bytes 10616832 | tf_op jit(solution)/shard_map/reduce_scatter | solution.py:173
  495.3 485.9 %all-reduce.4.cloned.1.call-start = ((), (), s32[]{:S(2)}) async-start(), calls=%async_computation.13 | async-start | bytes 3833856 | tf_op jit(solution)/shard_map/psum | solution.py:208
  500.5 431.3 %copy-start.5 = (f32[1024,768]{1,0:T(8,128)S(1)}, f32[1024,768]{1,0:T(8,128)}, u32[]{:S(2)}) copy-start(f32[1024,768]{1,0:T(8,128)} %copy-done.4) | copy-start | bytes 9437188
  500.5 431.3 %copy-start.25 = (f32[1024]{0:T(1024)S(1)}, f32[1024]{0:T(1024)}, u32[]{:S(2)}) copy-start(f32[1024]{0:T(1024)} %copy-done.24) | copy-start | bytes 12292
  (27 other events, 54.3 us)
Sparse Core Ops, SparseCore 0:
  10.2 148.5 all-gather.4
  161.0 39.2 all-gather.6
  202.5 78.0 all-gather.8
  282.6 77.6 all-gather.10
  388.7 68.0 reduce-scatter.6
  471.2 128.6 reduce-scatter.12
  603.5 161.2 reduce-scatter.8
  768.4 161.1 reduce-scatter.10
  933.4 47.7 all-reduce.3
